TPU v7x, 128 devices: a whole 4x4x4 slice. The times are simulated.
128 devices in a mesh: date: 2 (over core), space: 64 (over z, y, x).
Axes of the slice: x: 4, y: 4, z: 4, core: 2. Of those that a mesh axis runs over, the one named last changes fastest.
Arguments:
- acquisitions: bfloat16 [16, 8192, 512], P('date', 'space')
- partner: int32 [16, 9], replicated, may hold values from 0 to 15, as said below
- pair_count: int32 [16], replicated, may hold values from 2 to 9, as said below
- band_low: int32 [16, 9], P('date'), may hold values from 0 to 95
- band_high: int32 [16, 9], P('date'), may hold values from 160 to 256
Outputs:
- coherence: bfloat16 [16, 9, 8192, 512], P('date', None, 'space')
Inputs may be any that keep to these rules, and one draw needn't show every extreme that they name: For j < pair_count[d], partner[d, j] is the secondary date of pair j of date d; other slots name any date but no pair. A secondary never lies in its reference's block of 8 dates (one index of date), and the pairs of one block name at most 4 distinct dates of any other block; some two blocks reach 4. The pairs of date d are its first pair_count[d] slots.
All inputs are finite; a program needn't handle non-finite values.
Results may differ from a plain program's by a relative error of at most 0.0085.
Values may be sent and summed in bfloat16 or wider, within the bound.
A program may use at most 192 MiB of HBM per device.

v0:
```python
import functools
import math

import jax
import jax.numpy as jnp
import numpy as np
from jax import lax
from jax.experimental import pallas as pl
from jax.experimental.pallas import tpu as pltpu
from jax.sharding import PartitionSpec as P

F32 = jnp.float32
BF16 = jnp.bfloat16


def tables(bins):
    ids = np.arange(bins)
    angles = (ids[:, None] * ids[None, :] % bins) * (2.0 * math.pi / bins)
    cosine, sine = np.cos(angles), np.sin(angles)
    forward = np.block([[cosine, -sine], [sine, cosine]])
    inverse = np.block([[cosine, sine], [-sine, cosine]]) / bins
    half = bins // 2
    rows = np.concatenate([np.arange(half), bins + np.arange(half)])
    even = np.concatenate([np.arange(0, bins, 2), bins + np.arange(0, bins, 2)])
    odd = even + 1
    order = np.concatenate([np.arange(0, bins, 2), np.arange(1, bins, 2)])
    window = (np.abs(order[:, None] - ids[None, :]) <= 4).astype(np.float32)
    return (
        jnp.asarray(forward, BF16),
        jnp.asarray(inverse[rows][:, even], BF16),
        jnp.asarray(inverse[rows][:, odd], BF16),
        jnp.asarray(window, BF16),
    )


def exchange_kernel(
    acq_ref, fwd_ref, spec_ref, other, edge_f, edge, halo, halo_f, grid_f, send, recv
):
    dates, rows, cols = acq_ref.shape
    quarters = cols // 128
    date = lax.axis_index("date")
    space = lax.axis_index("space")
    count = lax.axis_size("space")
    before = lax.rem(space + count - 1, count)
    after = lax.rem(space + 1, count)
    far = 1 - date

    barrier = pltpu.get_barrier_semaphore()
    peers = ((far, space), (date, before), (date, after), (far, before), (far, after))
    for peer in peers:
        pl.semaphore_signal(barrier, inc=1, device_id=peer, device_id_type=pl.DeviceIdType.MESH)
    for d in range(dates):
        edge_f[0, d : d + 1, :] = acq_ref[d, 0:16, :].astype(F32)[0:1]
        edge_f[1, d : d + 1, :] = acq_ref[d, rows - 16 : rows, :].astype(F32)[15:16]
    edge[...] = edge_f[...].astype(BF16)
    pl.semaphore_wait(barrier, len(peers))

    def remote(src, dst, k, peer):
        copy = pltpu.make_async_remote_copy(
            src_ref=src,
            dst_ref=dst,
            send_sem=send.at[k],
            recv_sem=recv.at[k],
            device_id=peer,
            device_id_type=pl.DeviceIdType.MESH,
        )
        copy.start()
        return copy

    small = [
        remote(edge.at[1], halo.at[0], 0, (date, after)),
        remote(edge.at[0], halo.at[1], 1, (date, before)),
        remote(edge.at[1], halo.at[2], 2, (far, after)),
        remote(edge.at[0], halo.at[3], 3, (far, before)),
    ]
    big = remote(acq_ref, other, 4, (far, space))

    for copy in small:
        copy.wait()
    top = (space > 0).astype(F32)
    bottom = (space < count - 1).astype(F32)
    for k in range(4):
        block = jnp.dot(halo[k], fwd_ref[...], preferred_element_type=F32)
        halo_f[k] = block * (top if k % 2 == 0 else bottom)

    def place(source, base, halo_base):
        @pl.loop(0, dates)
        def _(i):
            block = jnp.dot(source[i], fwd_ref[...], preferred_element_type=F32)
            first = halo_f[halo_base, pl.ds(i, 1), :]
            last = halo_f[halo_base + 1, pl.ds(i, 1), :]
            for q in range(quarters):
                span = slice(q * 128, q * 128 + 128)
                grid_f[q, 8 : 8 + rows, :] = block[:, span]
                grid_f[q, 7:8, :] = first[:, span]
                grid_f[q, 8 + rows : 9 + rows, :] = last[:, span]
            for q in range(quarters):
                span = slice(q * 128, q * 128 + 128)
                for t in range(10):
                    low = grid_f[q, pl.ds(7 + t, 8, stride=8), :]
                    high = grid_f[q, pl.ds(71 + t, 8, stride=8), :]
                    tile = jnp.concatenate([low, high], 0).astype(BF16)
                    spec_ref[base + i, t * 16 : t * 16 + 16, span] = tile

    place(acq_ref, 0, 0)
    big.wait()
    place(other, dates, 2)


def pair_kernel(
    partner_ref, count_ref, low_ref, high_ref, spec_ref, even_ref, odd_ref, win_ref, out_ref, grid_f
):
    date = pl.program_id(0)
    dates = pl.num_programs(0)
    slots = out_ref.shape[1]
    mine = lax.axis_index("date") * dates + date
    live_count = count_ref[mine]
    lane = lax.broadcasted_iota(jnp.int32, (16, 128), 1)

    for j in range(slots):
        live = j < live_count
        low = jnp.where(live, low_ref[date, j], 512)
        high = high_ref[date, j]
        second = dates + lax.rem(partner_ref[mine, j], dates)
        mask_lo = ((lane >= low) & (lane < high)).astype(F32).astype(BF16)[None]
        mask_hi = ((lane + 128 >= low) & (lane + 128 < high)).astype(F32).astype(BF16)[None]
        plus, minus = [], []
        for index in (date, second):
            x = [
                spec_ref[index, :, q * 128 : q * 128 + 128].reshape(10, 16, 128)
                * (mask_lo if q % 2 == 0 else mask_hi)
                for q in range(4)
            ]
            plus.append(
                jnp.concatenate([(x[0] + x[1]).reshape(160, 128), (x[2] + x[3]).reshape(160, 128)], 1)
            )
            minus.append(
                jnp.concatenate([(x[0] - x[1]).reshape(160, 128), (x[2] - x[3]).reshape(160, 128)], 1)
            )
        fields = []
        for part, table in ((plus, even_ref), (minus, odd_ref)):
            both = jnp.dot(
                jnp.concatenate(part, 0), table[...], preferred_element_type=F32
            ).astype(BF16)
            ar, ai = both[:160, :128], both[:160, 128:]
            br, bi = both[160:, :128], both[160:, 128:]
            raw = [ar * br + ai * bi, ai * br - ar * bi, ar * ar + ai * ai, br * br + bi * bi]
            summed = []
            for f in raw:
                f = f.reshape(10, 16, 128)
                summed.append((f[0:8] + f[1:9] + f[2:10]).reshape(128, 128))
            fields.append(jnp.concatenate(summed, 0))
        looked = jnp.dot(
            jnp.concatenate(fields, 1), win_ref[...], preferred_element_type=F32
        )
        norm = lax.rsqrt(jnp.maximum(looked[256:384], 1.0) * jnp.maximum(looked[384:512], 1.0))
        for c in range(2):
            value = looked[c * 128 : c * 128 + 128] * norm
            for h in range(2):
                q = 2 * c + h
                span = slice(h * 128, h * 128 + 128)
                for t in range(8):
                    for g in range(2):
                        tile = value[t * 16 + g * 8 : t * 16 + g * 8 + 8, span]
                        grid_f[j % 2, q, pl.ds(64 * g + t, 8, stride=8), :] = tile
                out_ref[0, j, :, q * 128 : q * 128 + 128] = grid_f[j % 2, q].astype(BF16)


def local(acquisitions, partner, pair_count, band_low, band_high):
    dates, rows, cols = acquisitions.shape
    slots = partner.shape[1]
    forward, even, odd, window = tables(cols // 2)
    vmem = pl.BlockSpec(memory_space=pltpu.VMEM)
    smem = pl.BlockSpec(memory_space=pltpu.SMEM)
    spectra = pl.pallas_call(
        exchange_kernel,
        out_shape=jax.ShapeDtypeStruct((2 * dates, 160, cols), BF16),
        in_specs=[vmem, vmem],
        out_specs=vmem,
        scratch_shapes=[
            pltpu.VMEM((dates, rows, cols), BF16),
            pltpu.VMEM((2, dates, cols), F32),
            pltpu.VMEM((2, dates, cols), BF16),
            pltpu.VMEM((4, dates, cols), BF16),
            pltpu.VMEM((4, dates, cols), F32),
            pltpu.VMEM((cols // 128, rows + 16, 128), F32),
            pltpu.SemaphoreType.DMA((5,)),
            pltpu.SemaphoreType.DMA((5,)),
        ],
        compiler_params=pltpu.CompilerParams(
            collective_id=0, has_side_effects=True, vmem_limit_bytes=32 << 20
        ),
        name="exchange",
    )(acquisitions, forward)
    return pl.pallas_call(
        pair_kernel,
        grid=(dates,),
        out_shape=jax.ShapeDtypeStruct((dates, slots, rows, cols), BF16),
        in_specs=[smem, smem, smem, smem, vmem, vmem, vmem, vmem],
        out_specs=pl.BlockSpec((1, slots, rows, cols), lambda d: (d, 0, 0, 0)),
        scratch_shapes=[pltpu.VMEM((2, cols // 128, rows, 128), F32)],
        compiler_params=pltpu.CompilerParams(vmem_limit_bytes=40 << 20),
        name="pairs",
    )(partner, pair_count, band_low, band_high, spectra, even, odd, window)


def solution(mesh):
    placed = (P("date", "space", None), P(), P(), P("date", None), P("date", None))
    return jax.shard_map(
        local, mesh=mesh, in_specs=placed, out_specs=P("date", None, "space", None), check_vma=False
    )
```

profile of v0, /device:TPU:1, one launch (start us, length us, event | category | flops | bytes accessed | tf_op | source)
XLA Modules:
  0.0 52.4 jit_solution(7318175037848024845)
XLA Ops:
  0.0 0.0 copy-start
  0.0 1.2 %copy-done = bf16[8,128,512]{2,1,0:T(8,128)(2,1)S(1)} copy-done((bf16[8,128,512]{2,1,0:T(8,128)(2,1)S(1)}, bf16[8,128,512]{2,1,0:T(8,128)(2,1)}, u32[]{:S(2)}) %copy-start) | copy-done | bytes 1048600
  1.2 0.0 copy-start.1
  1.2 1.0 %copy-done.1 = bf16[512,512]{1,0:T(8,128)(2,1)S(1)} copy-done((bf16[512,512]{1,0:T(8,128)(2,1)S(1)}, bf16[512,512]{1,0:T(8,128)(2,1)}, u32[]{:S(2)}) %copy-start.1) | copy-done | bytes 524312
  2.3 17.3 %exchange.1.spec_ref = bf16[16,160,512]{2,1,0:T(8,128)(2,1)S(1)} custom-call(bf16[8,128,512]{2,1,0:T(8,128)(2,1)S(1)} %copy-done, bf16[512,512]{1,0:T(8,128)(2,1)S(1)} %copy-done.1), custom_call_target="tpu_custom_call" | custom-call | tf_op jit(solution)/shard_map/exchange/pallas_call | solution.py:175
  19.6 0.0 copy-start.2
  19.6 0.9 %copy-done.2 = bf16[256,256]{1,0:T(8,128)(2,1)S(1)} copy-done((bf16[256,256]{1,0:T(8,128)(2,1)S(1)}, bf16[256,256]{1,0:T(8,128)(2,1)}, u32[]{:S(2)}) %copy-start.2) | copy-done | bytes 131096
  20.5 0.0 copy-start.3
  20.5 0.9 %copy-done.3 = bf16[256,256]{1,0:T(8,128)(2,1)S(1)} copy-done((bf16[256,256]{1,0:T(8,128)(2,1)S(1)}, bf16[256,256]{1,0:T(8,128)(2,1)}, u32[]{:S(2)}) %copy-start.3) | copy-done | bytes 131096
  21.4 0.0 copy-start.4
  21.4 0.9 %copy-done.4 = bf16[256,256]{1,0:T(8,128)(2,1)S(1)} copy-done((bf16[256,256]{1,0:T(8,128)(2,1)S(1)}, bf16[256,256]{1,0:T(8,128)(2,1)}, u32[]{:S(2)}) %copy-start.4) | copy-done | bytes 131096
  22.3 0.0 copy-start.5
  22.3 0.7 %copy-done.5 = s32[16,9]{1,0:T(8,128)S(1)} copy-done((s32[16,9]{1,0:T(8,128)S(1)}, s32[16,9]{1,0:T(8,128)}, u32[]{:S(2)}) %copy-start.5) | copy-done | bytes 600
  23.0 0.0 copy-start.6
  23.0 0.7 %copy-done.6 = s32[8,9]{1,0:T(8,128)S(1)} copy-done((s32[8,9]{1,0:T(8,128)S(1)}, s32[8,9]{1,0:T(8,128)}, u32[]{:S(2)}) %copy-start.6) | copy-done | bytes 312
  23.7 0.0 copy-start.7
  23.7 0.7 %copy-done.7 = s32[8,9]{1,0:T(8,128)S(1)} copy-done((s32[8,9]{1,0:T(8,128)S(1)}, s32[8,9]{1,0:T(8,128)}, u32[]{:S(2)}) %copy-start.7) | copy-done | bytes 312
  24.4 0.0 copy-start.8
  24.4 0.7 %copy-done.8 = s32[16]{0:T(128)S(1)} copy-done((s32[16]{0:T(128)S(1)}, s32[16]{0:T(128)}, u32[]{:S(2)}) %copy-start.8) | copy-done | bytes 88
  25.1 27.3 %pairs.1 = bf16[8,9,128,512]{3,2,1,0:T(8,128)(2,1)} custom-call(s32[16,9]{1,0:T(8,128)S(1)} %copy-done.5, s32[16]{0:T(128)S(1)} %copy-done.8, s32[8,9]{1,0:T(8,128)S(1)} %copy-done.6, s32[8,9]{1,0:T(8,128)S(1)} %copy-done.7, bf16[16,160,512]{2,1,0:T(8,128)(2,1)S(1)} %exchange.1.spec_ref, bf16[256,256]{1,0:T(8,128)(2,1)S(1)} %copy-done.4, ...), custom_call_target="tpu_custom_call" | custom-call | tf_op jit(solution)/shard_map/pairs/pallas_call | solution.py:195
Async XLA Ops:
  0.0 1.2 %copy-start = (bf16[8,128,512]{2,1,0:T(8,128)(2,1)S(1)}, bf16[8,128,512]{2,1,0:T(8,128)(2,1)}, u32[]{:S(2)}) copy-start(bf16[8,128,512]{2,1,0:T(8,128)(2,1)} %acq_ref.1) | copy-start | bytes 3145732
  1.2 1.0 %copy-start.1 = (bf16[512,512]{1,0:T(8,128)(2,1)S(1)}, bf16[512,512]{1,0:T(8,128)(2,1)}, u32[]{:S(2)}) copy-start(bf16[512,512]{1,0:T(8,128)(2,1)} %constant.8.clone.fwd_ref) | copy-start | bytes 1572868
  19.6 0.9 %copy-start.2 = (bf16[256,256]{1,0:T(8,128)(2,1)S(1)}, bf16[256,256]{1,0:T(8,128)(2,1)}, u32[]{:S(2)}) copy-start(bf16[256,256]{1,0:T(8,128)(2,1)} %constant.11.clone.win_ref) | copy-start | bytes 393220
  20.5 0.9 %copy-start.3 = (bf16[256,256]{1,0:T(8,128)(2,1)S(1)}, bf16[256,256]{1,0:T(8,128)(2,1)}, u32[]{:S(2)}) copy-start(bf16[256,256]{1,0:T(8,128)(2,1)} %constant.10.clone.odd_ref) | copy-start | bytes 393220
  21.4 0.9 %copy-start.4 = (bf16[256,256]{1,0:T(8,128)(2,1)S(1)}, bf16[256,256]{1,0:T(8,128)(2,1)}, u32[]{:S(2)}) copy-start(bf16[256,256]{1,0:T(8,128)(2,1)} %constant.9.clone.even_ref) | copy-start | bytes 393220
  22.3 0.7 %copy-start.5 = (s32[16,9]{1,0:T(8,128)S(1)}, s32[16,9]{1,0:T(8,128)}, u32[]{:S(2)}) copy-start(s32[16,9]{1,0:T(8,128)} %partner_ref.1) | copy-start | bytes 1732
  23.0 0.7 %copy-start.6 = (s32[8,9]{1,0:T(8,128)S(1)}, s32[8,9]{1,0:T(8,128)}, u32[]{:S(2)}) copy-start(s32[8,9]{1,0:T(8,128)} %low_ref.1) | copy-start | bytes 868
  23.7 0.7 %copy-start.7 = (s32[8,9]{1,0:T(8,128)S(1)}, s32[8,9]{1,0:T(8,128)}, u32[]{:S(2)}) copy-start(s32[8,9]{1,0:T(8,128)} %high_ref.1) | copy-start | bytes 868
  24.4 0.7 %copy-start.8 = (s32[16]{0:T(128)S(1)}, s32[16]{0:T(128)}, u32[]{:S(2)}) copy-start(s32[16]{0:T(128)} %count_ref.1) | copy-start | bytes 196
where the time goes:
time: 52.7 us; the launch traced here: 52.4 us
  Pallas kernels  44.7 us (85%)
  local copies, waits for them, and re-layouts  7.7 us (15%)
    pallas_call x1, Pallas kernels, local(): pl.pallas_call(pair_kernel, grid=(dates,), out_shape=jax.ShapeDtypeStruct...  27.3 us
    pallas_call x1, Pallas kernels, local(): pl.pallas_call(exchange_kernel, out_shape=jax.ShapeDtypeStruct((2 * dates...  17.3 us
    unnamed x18, local copies, waits for them, and re-layouts  7.7 us

commit v1 on v0

v1 whole, which is shorter than its diff:
```python
import functools
import math

import jax
import jax.numpy as jnp
import numpy as np
from jax import lax
from jax.experimental import pallas as pl
from jax.experimental.pallas import tpu as pltpu
from jax.sharding import PartitionSpec as P

F32 = jnp.float32
BF16 = jnp.bfloat16


def tables(bins):
    ids = np.arange(bins)
    angles = (ids[:, None] * ids[None, :] % bins) * (2.0 * math.pi / bins)
    cosine, sine = np.cos(angles), np.sin(angles)
    forward = np.block([[cosine, -sine], [sine, cosine]])
    inverse = np.block([[cosine, sine], [-sine, cosine]]) / bins
    half = bins // 2
    rows = np.concatenate([np.arange(half), bins + np.arange(half)])
    even = np.concatenate([np.arange(0, bins, 2), bins + np.arange(0, bins, 2)])
    odd = even + 1
    order = np.concatenate([np.arange(0, bins, 2), np.arange(1, bins, 2)])
    window = (np.abs(order[:, None] - ids[None, :]) <= 4).astype(np.float32)
    return (
        jnp.asarray(forward, BF16),
        jnp.asarray(inverse[rows][:, even], BF16),
        jnp.asarray(inverse[rows][:, odd], BF16),
        jnp.asarray(window, BF16),
    )


BASE = 16
PITCH = 9
MESH = pl.DeviceIdType.MESH


def segment(ref, lead, t):
    shift = {-1: -2, 8: PITCH}.get(t, t)
    parts = [ref[lead + (pl.ds(BASE + 8 * PITCH * h + shift, 8, stride=PITCH),)] for h in range(2)]
    return jnp.concatenate(parts, 0)


def band(low, high, live):
    lane = lax.broadcasted_iota(jnp.int32, (16, 128), 1)
    low = jnp.where(live, low, 512)
    return [
        ((lane + shift >= low) & (lane + shift < high)).astype(F32).astype(BF16)
        for shift in (0, 128)
    ]


def halves(tile, masks):
    x = [tile[q] * masks[q % 2] for q in range(4)]
    return (
        jnp.concatenate([x[0] + x[1], x[2] + x[3]], 1),
        jnp.concatenate([x[0] - x[1], x[2] - x[3]], 1),
    )


def front_kernel(
    acq_hbm, fwd_hbm, even_hbm, odd_hbm, low_hbm, high_hbm, count_hbm,
    far_ref, ref_ref,
    own, other, fwd, even, odd, low_s, high_s, count_s,
    edge_f, edge, halo, halo_f, nat, local_sem, send, recv,
):
    dates, rows, cols = own.shape
    slots = low_s.shape[1]
    quarters = cols // 128
    date = lax.axis_index("date")
    space = lax.axis_index("space")
    count = lax.axis_size("space")
    before = lax.rem(space + count - 1, count)
    after = lax.rem(space + 1, count)
    far = 1 - date
    has_before = space > 0
    has_after = space < count - 1

    barrier = pltpu.get_barrier_semaphore()

    def greet(peer):
        pl.semaphore_signal(barrier, inc=1, device_id=peer, device_id_type=MESH)

    greet((far, space))

    @pl.when(has_before)
    def _():
        greet((date, before))
        greet((far, before))

    @pl.when(has_after)
    def _():
        greet((date, after))
        greet((far, after))

    loads = [
        pltpu.make_async_copy(src, dst, local_sem.at[k])
        for k, (src, dst) in enumerate(
            (
                (acq_hbm, own),
                (fwd_hbm, fwd),
                (even_hbm, even),
                (odd_hbm, odd),
                (low_hbm, low_s),
                (high_hbm, high_s),
                (count_hbm, count_s),
            )
        )
    ]
    for load in loads:
        load.start()

    def remote(src, dst, k, peer):
        return pltpu.make_async_remote_copy(
            src_ref=src,
            dst_ref=dst,
            send_sem=send.at[k],
            recv_sem=recv.at[k],
            device_id=peer,
            device_id_type=MESH,
        )

    down = [remote(edge.at[1], halo.at[0], 0, (date, after)), remote(edge.at[1], halo.at[2], 2, (far, after))]
    up = [remote(edge.at[0], halo.at[1], 1, (date, before)), remote(edge.at[0], halo.at[3], 3, (far, before))]
    big = remote(own, other, 4, (far, space))

    loads[0].wait()
    for d in range(dates):
        edge_f[0, d : d + 1, :] = own[d, 0:16, :].astype(F32)[0:1]
        edge_f[1, d : d + 1, :] = own[d, rows - 16 : rows, :].astype(F32)[15:16]
    edge[...] = edge_f[...].astype(BF16)

    pl.semaphore_wait(
        barrier, 1 + 2 * has_before.astype(jnp.int32) + 2 * has_after.astype(jnp.int32)
    )
    big.start()

    @pl.when(has_after)
    def _():
        for copy in down:
            copy.start()

    @pl.when(has_before)
    def _():
        for copy in up:
            copy.start()

    def transform(source, i):
        block = jnp.dot(source[i], fwd[...], preferred_element_type=F32)
        for q in range(quarters):
            for s in range(rows // 8):
                place = slice(BASE + PITCH * s, BASE + PITCH * s + 8)
                nat[i, q, place, :] = block[8 * s : 8 * s + 8, q * 128 : q * 128 + 128]

    def references(i, tiles):
        x = [[segment(nat, (i, q), t).astype(BF16) for q in range(quarters)] for t in tiles]
        plus, minus = [], []
        first = date * dates
        for j in range(slots):
            masks = band(low_s[i, j], high_s[i, j], j < count_s[first + i])
            for tile in x:
                p, m = halves(tile, masks)
                plus.append(p)
                minus.append(m)
        for e, (part, table) in enumerate(((plus, even), (minus, odd))):
            both = jnp.dot(jnp.concatenate(part, 0), table[...], preferred_element_type=F32)
            for j in range(slots):
                for k, t in enumerate(tiles):
                    top = 16 * (j * len(tiles) + k)
                    for c in range(2):
                        ref_ref[i * slots + j, t + 1, e, c] = both[top : top + 16, 128 * c : 128 * c + 128]

    for load in loads[1:]:
        load.wait()

    @pl.loop(0, dates)
    def _(i):
        transform(own, i)

    @pl.loop(0, dates)
    def _(i):
        references(i, tuple(range(8)))

    @pl.when(has_after)
    def _():
        for copy in down:
            copy.wait_send()
        for copy in up:
            copy.wait_recv()

    @pl.when(has_before)
    def _():
        for copy in up:
            copy.wait_send()
        for copy in down:
            copy.wait_recv()

    @pl.when(jnp.logical_not(has_before))
    def _():
        halo[0] = jnp.zeros(halo.shape[1:], BF16)
        halo[2] = jnp.zeros(halo.shape[1:], BF16)

    @pl.when(jnp.logical_not(has_after))
    def _():
        halo[1] = jnp.zeros(halo.shape[1:], BF16)
        halo[3] = jnp.zeros(halo.shape[1:], BF16)

    for k in range(4):
        halo_f[k] = jnp.dot(halo[k], fwd[...], preferred_element_type=F32)

    def fringe(k):
        for i in range(dates):
            for q in range(quarters):
                span = slice(q * 128, q * 128 + 128)
                nat[i, q, BASE - 2 : BASE - 1, :] = halo_f[k, i : i + 1, span]
                nat[i, q, BASE + 16 * PITCH : BASE + 16 * PITCH + 1, :] = halo_f[k + 1, i : i + 1, span]

    fringe(0)

    @pl.loop(0, dates)
    def _(i):
        references(i, (-1, 8))

    fringe(2)
    big.wait()

    @pl.loop(0, dates)
    def _(i):
        transform(other, i)
        for q in range(quarters):
            for t in range(-1, 9):
                far_ref[i, q, 16 * t + 16 : 16 * t + 32, :] = segment(nat, (i, q), t)


def pair_kernel(
    far_ref, ref_ref, even_hbm, odd_hbm, win_hbm, partner_hbm, low_hbm, high_hbm, count_hbm,
    out_ref,
    even, odd, win, partner_s, low_s, high_s, count_s, sec0, sec1, grid0, grid1, ready, local_sem, out_sem,
):
    dates, slots = low_s.shape
    pairs = dates * slots
    depth = ready.shape[0]
    unroll = depth // 2
    first = lax.axis_index("date") * dates
    loads = [
        pltpu.make_async_copy(src, dst, local_sem.at[k])
        for k, (src, dst) in enumerate(
            (
                (even_hbm, even),
                (odd_hbm, odd),
                (win_hbm, win),
                (partner_hbm, partner_s),
                (low_hbm, low_s),
                (high_hbm, high_s),
                (count_hbm, count_s),
            )
        )
    ]
    for load in loads:
        load.start()

    def finish(p, slot):
        return pltpu.make_async_copy(
            ready.at[slot], out_ref.at[p // slots, lax.rem(p, slots)], out_sem.at[slot]
        )

    for s in range(depth):
        finish(s, s).start()
    for load in loads:
        load.wait()

    def secondary(p, buf):
        d = p // slots
        j = p - d * slots
        masks = band(low_s[d, j], high_s[d, j], j < count_s[first + d])
        index = lax.rem(partner_s[first + d, j], dates)
        plus, minus = [], []
        for t in range(10):
            tile = [far_ref[index, q, 16 * t : 16 * t + 16, :].astype(BF16) for q in range(4)]
            a, b = halves(tile, masks)
            plus.append(a)
            minus.append(b)
        for e, (part, table) in enumerate(((plus, even), (minus, odd))):
            both = jnp.dot(jnp.concatenate(part, 0), table[...], preferred_element_type=F32)
            for t in range(10):
                for c in range(2):
                    buf[t, e, c] = both[16 * t : 16 * t + 16, 128 * c : 128 * c + 128]

    def coherence(p, buf, grid, slot):
        lines, tiles = [], []
        for t in range(10):
            fields = [[], [], [], []]
            for e in range(2):
                ar, ai = (ref_ref[p, t, e, c].astype(BF16) for c in range(2))
                br, bi = (buf[t, e, c].astype(BF16) for c in range(2))
                fields[0].append(ar * br + ai * bi)
                fields[1].append(ai * br - ar * bi)
                fields[2].append(ar * ar + ai * ai)
                fields[3].append(br * br + bi * bi)
            tiles.append(fields)
            if t >= 2:
                for k in range(4):
                    three = [tiles[t - 2][k][e] + tiles[t - 1][k][e] + tiles[t][k][e] for e in range(2)]
                    lines.append(jnp.concatenate(three, 1))
        looked = jnp.dot(jnp.concatenate(lines, 0), win[...], preferred_element_type=F32)
        for t in range(8):
            cr, ci, pr, ps = (looked[64 * t + 16 * k : 64 * t + 16 * k + 16] for k in range(4))
            norm = lax.rsqrt(jnp.maximum(pr, 1.0) * jnp.maximum(ps, 1.0))
            for c, v in ((0, cr), (1, ci)):
                v = v * norm
                for h in range(2):
                    for g in range(2):
                        where = pl.ds(8 * PITCH * g + t, 8, stride=PITCH)
                        grid[2 * c + h, where, :] = v[8 * g : 8 * g + 8, 128 * h : 128 * h + 128]
        for q in range(4):
            for s in range(8):
                v = [grid[q, pl.ds(PITCH * (2 * s + g), 8), :] for g in range(2)]
                ready[slot, 16 * s : 16 * s + 16, 128 * q : 128 * q + 128] = jnp.concatenate(v, 0).astype(BF16)

    secs, grids = (sec0, sec1), (grid0, grid1)
    secondary(0, sec0)

    @pl.loop(0, pairs // unroll)
    def _(i):
        base = unroll * i
        at = [lax.rem(base + u, depth) for u in range(unroll)]
        for u in range(unroll):
            finish(base + u, at[u]).wait()
        for u in range(unroll):
            following = base + u + 1
            if u == unroll - 1:
                following = jnp.minimum(following, pairs - 1)
            secondary(following, secs[(u + 1) % 2])
            coherence(base + u, secs[u % 2], grids[u % 2], at[u])
        for u in range(unroll):
            finish(base + u, at[u]).start()

    for s in range(depth):
        finish(s, s).wait()


def local(acquisitions, partner, pair_count, band_low, band_high):
    dates, rows, cols = acquisitions.shape
    slots = partner.shape[1]
    quarters = cols // 128
    unroll = 8
    forward, even, odd, window = tables(cols // 2)
    vmem = pl.BlockSpec(memory_space=pltpu.VMEM)
    hbm = pl.BlockSpec(memory_space=pltpu.HBM)
    stay = functools.partial(pltpu.with_memory_space_constraint, memory_space=pltpu.HBM)
    forward, even, odd, window, acquisitions, partner, pair_count, band_low, band_high = (
        stay(x)
        for x in (forward, even, odd, window, acquisitions, partner, pair_count, band_low, band_high)
    )
    half = pltpu.VMEM((256, 256), BF16)
    per_slot = pltpu.SMEM((dates, slots), jnp.int32)
    far, ref = pl.pallas_call(
        front_kernel,
        out_shape=(
            jax.ShapeDtypeStruct((dates, quarters, 160, 128), F32),
            jax.ShapeDtypeStruct((dates * slots, 10, 2, 2, 16, 128), F32),
        ),
        in_specs=[hbm] * 7,
        out_specs=(vmem, vmem),
        scratch_shapes=[
            pltpu.VMEM((dates, rows, cols), BF16),
            pltpu.VMEM((dates, rows, cols), BF16),
            pltpu.VMEM((cols, cols), BF16),
            half,
            half,
            per_slot,
            per_slot,
            pltpu.SMEM(pair_count.shape, jnp.int32),
            pltpu.VMEM((2, dates, cols), F32),
            pltpu.VMEM((2, dates, cols), BF16),
            pltpu.VMEM((4, dates, cols), BF16),
            pltpu.VMEM((4, dates, cols), F32),
            pltpu.VMEM((dates, quarters, BASE + 16 * PITCH + 8, 128), F32),
            pltpu.SemaphoreType.DMA((7,)),
            pltpu.SemaphoreType.DMA((5,)),
            pltpu.SemaphoreType.DMA((5,)),
        ],
        compiler_params=pltpu.CompilerParams(
            collective_id=0, has_side_effects=True, vmem_limit_bytes=16 << 20
        ),
        name="front",
    )(acquisitions, forward, even, odd, band_low, band_high, pair_count)
    return pl.pallas_call(
        pair_kernel,
        out_shape=jax.ShapeDtypeStruct((dates, slots, rows, cols), BF16),
        in_specs=[vmem, vmem] + [hbm] * 7,
        out_specs=hbm,
        scratch_shapes=[
            half,
            half,
            half,
            pltpu.SMEM(partner.shape, jnp.int32),
            per_slot,
            per_slot,
            pltpu.SMEM(pair_count.shape, jnp.int32),
            pltpu.VMEM((10, 2, 2, 16, 128), F32),
            pltpu.VMEM((10, 2, 2, 16, 128), F32),
            pltpu.VMEM((quarters, 160, 128), F32),
            pltpu.VMEM((quarters, 160, 128), F32),
            pltpu.VMEM((2 * unroll, rows, cols), BF16),
            pltpu.SemaphoreType.DMA((7,)),
            pltpu.SemaphoreType.DMA((2 * unroll,)),
        ],
        compiler_params=pltpu.CompilerParams(vmem_limit_bytes=16 << 20),
        name="pairs",
    )(far, ref, even, odd, window, partner, band_low, band_high, pair_count)


def solution(mesh):
    placed = (P("date", "space", None), P(), P(), P("date", None), P("date", None))
    return jax.shard_map(
        local, mesh=mesh, in_specs=placed, out_specs=P("date", None, "space", None), check_vma=False
    )
```

time: 52.7 us -> 32.4 us (0.61)
  the two profiles are of different devices: /device:TPU:1 before, /device:TPU:97 now
where the time goes in v1:
time: 32.4 us; the launch traced here: 32.2 us
  Pallas kernels  32.2 us (99%)
    pallas_call x1, Pallas kernels, local(): pl.pallas_call(pair_kernel, out_shape=jax.ShapeDtypeStruct((dates, slots,...  16.7 us
    pallas_call x1, Pallas kernels, local(): pl.pallas_call(front_kernel, out_shape=(jax.ShapeDtypeStruct((dates, quar...  15.6 us

profile of v1, /device:TPU:97, one launch (start us, length us, event | category | flops | bytes accessed | tf_op | source)
XLA Modules:
  0.0 32.2 jit_solution(9173083356038141473)
XLA Ops:
  0.0 15.6 %front.1 = (f32[8,4,160,128]{3,2,1,0:T(8,128)S(1)}, f32[72,10,2,2,16,128]{5,4,3,2,1,0:T(8,128)S(1)}) custom-call(bf16[8,128,512]{2,1,0:T(8,128)(2,1)} %acq_hbm.1, bf16[512,512]{1,0:T(8,128)(2,1)} %constant.8.clone.fwd_hbm, bf16[256,256]{1,0:T(8,128)(2,1)} %constant.9.clone.even_hbm, bf16[256,256]{1,0:T(8,128)(2,1)} %constant.10.clone.odd_hbm, ...), custom_call_target="tpu_custom_call" | custom-call | tf_op jit(solution)/shard_map/front/pallas_call | solution.py:360
  15.6 16.7 %pairs.1 = bf16[8,9,128,512]{3,2,1,0:T(8,128)(2,1)} custom-call(f32[8,4,160,128]{3,2,1,0:T(8,128)S(1)} %get-tuple-element.7.far_ref, f32[72,10,2,2,16,128]{5,4,3,2,1,0:T(8,128)S(1)} %get-tuple-element.8.ref_ref, bf16[256,256]{1,0:T(8,128)(2,1)} %constant.9.clone.even_hbm, bf16[256,256]{1,0:T(8,128)(2,1)} %constant.10.clone.odd_hbm, ...), custom_call_target="tpu_custom_call" | custom-call | tf_op jit(solution)/shard_map/pairs/pallas_call | solution.py:391

commit v2 on v1

--- a/solution.py
+++ b/solution.py
@@ -65,7 +65,7 @@
     acq_hbm, fwd_hbm, even_hbm, odd_hbm, low_hbm, high_hbm, count_hbm,
     far_ref, ref_ref,
     own, other, fwd, even, odd, low_s, high_s, count_s,
-    edge_f, edge, halo, halo_f, nat, local_sem, send, recv,
+    edge_f, edge, halo, halo_f, nat, nat_far, local_sem, send, recv,
 ):
     dates, rows, cols = own.shape
     slots = low_s.shape[1]
@@ -136,7 +136,6 @@
     pl.semaphore_wait(
         barrier, 1 + 2 * has_before.astype(jnp.int32) + 2 * has_after.astype(jnp.int32)
     )
-    big.start()
 
     @pl.when(has_after)
     def _():
@@ -148,41 +147,59 @@
         for copy in up:
             copy.start()
 
-    def transform(source, i):
-        block = jnp.dot(source[i], fwd[...], preferred_element_type=F32)
-        for q in range(quarters):
+    big.start()
+
+    def transform(source, target):
+        block = jnp.dot(
+            source[...].reshape(dates * rows, cols), fwd[...], preferred_element_type=F32
+        )
+        for i in range(dates):
             for s in range(rows // 8):
+                top = i * rows + 8 * s
                 place = slice(BASE + PITCH * s, BASE + PITCH * s + 8)
-                nat[i, q, place, :] = block[8 * s : 8 * s + 8, q * 128 : q * 128 + 128]
-
-    def references(i, tiles):
-        x = [[segment(nat, (i, q), t).astype(BF16) for q in range(quarters)] for t in tiles]
+                for q in range(quarters):
+                    target[i, q, place, :] = block[top : top + 8, q * 128 : q * 128 + 128]
+
+    def references(start, amount, tiles):
         plus, minus = [], []
-        first = date * dates
-        for j in range(slots):
-            masks = band(low_s[i, j], high_s[i, j], j < count_s[first + i])
-            for tile in x:
-                p, m = halves(tile, masks)
-                plus.append(p)
-                minus.append(m)
+        for n in range(amount):
+            i = start + n
+            x = [[segment(nat, (i, q), t).astype(BF16) for q in range(quarters)] for t in tiles]
+            for j in range(slots):
+                masks = band(low_s[i, j], high_s[i, j], j < count_s[date * dates + i])
+                for tile in x:
+                    p, m = halves(tile, masks)
+                    plus.append(p)
+                    minus.append(m)
         for e, (part, table) in enumerate(((plus, even), (minus, odd))):
             both = jnp.dot(jnp.concatenate(part, 0), table[...], preferred_element_type=F32)
-            for j in range(slots):
+            for n in range(amount * slots):
                 for k, t in enumerate(tiles):
-                    top = 16 * (j * len(tiles) + k)
+                    top = 16 * (n * len(tiles) + k)
                     for c in range(2):
-                        ref_ref[i * slots + j, t + 1, e, c] = both[top : top + 16, 128 * c : 128 * c + 128]
+                        ref_ref[start * slots + n, t + 1, e, c] = both[
+                            top : top + 16, 128 * c : 128 * c + 128
+                        ]
+
+    def spread(tiles):
+        @pl.loop(0, dates)
+        def _(i):
+            for q in range(quarters):
+                for t in tiles:
+                    far_ref[i, q, 16 * t + 16 : 16 * t + 32, :] = segment(nat_far, (i, q), t)
 
     for load in loads[1:]:
         load.wait()
 
-    @pl.loop(0, dates)
+    transform(own, nat)
+
+    @pl.loop(0, dates // 2)
     def _(i):
-        transform(own, i)
-
-    @pl.loop(0, dates)
-    def _(i):
-        references(i, tuple(range(8)))
+        references(2 * i, 2, tuple(range(8)))
+
+    big.wait()
+    transform(other, nat_far)
+    spread(tuple(range(8)))
 
     @pl.when(has_after)
     def _():
@@ -208,37 +225,28 @@
         halo[1] = jnp.zeros(halo.shape[1:], BF16)
         halo[3] = jnp.zeros(halo.shape[1:], BF16)
 
-    for k in range(4):
-        halo_f[k] = jnp.dot(halo[k], fwd[...], preferred_element_type=F32)
-
-    def fringe(k):
+    halo_f[...] = jnp.dot(
+        halo[...].reshape(4 * dates, cols), fwd[...], preferred_element_type=F32
+    ).reshape(4, dates, cols)
+    for k, target in ((0, nat), (2, nat_far)):
         for i in range(dates):
             for q in range(quarters):
                 span = slice(q * 128, q * 128 + 128)
-                nat[i, q, BASE - 2 : BASE - 1, :] = halo_f[k, i : i + 1, span]
-                nat[i, q, BASE + 16 * PITCH : BASE + 16 * PITCH + 1, :] = halo_f[k + 1, i : i + 1, span]
-
-    fringe(0)
-
-    @pl.loop(0, dates)
+                target[i, q, BASE - 2 : BASE - 1, :] = halo_f[k, i : i + 1, span]
+                target[i, q, BASE + 16 * PITCH : BASE + 16 * PITCH + 1, :] = halo_f[k + 1, i : i + 1, span]
+
+    @pl.loop(0, dates // 4)
     def _(i):
-        references(i, (-1, 8))
-
-    fringe(2)
-    big.wait()
-
-    @pl.loop(0, dates)
-    def _(i):
-        transform(other, i)
-        for q in range(quarters):
-            for t in range(-1, 9):
-                far_ref[i, q, 16 * t + 16 : 16 * t + 32, :] = segment(nat, (i, q), t)
+        references(4 * i, 4, (-1, 8))
+
+    spread((-1, 8))
 
 
 def pair_kernel(
     far_ref, ref_ref, even_hbm, odd_hbm, win_hbm, partner_hbm, low_hbm, high_hbm, count_hbm,
     out_ref,
-    even, odd, win, partner_s, low_s, high_s, count_s, sec0, sec1, grid0, grid1, ready, local_sem, out_sem,
+    even, odd, win, partner_s, low_s, high_s, count_s, sec0, sec1,
+    grid0, grid1, grid2, grid3, ready, local_sem, out_sem,
 ):
     dates, slots = low_s.shape
     pairs = dates * slots
@@ -262,13 +270,12 @@
     for load in loads:
         load.start()
 
-    def finish(p, slot):
+    def finish(group, half):
         return pltpu.make_async_copy(
-            ready.at[slot], out_ref.at[p // slots, lax.rem(p, slots)], out_sem.at[slot]
+            ready.at[pl.ds(unroll * half, unroll)], out_ref.at[pl.ds(unroll * group, unroll)], out_sem.at[half]
         )
 
-    for s in range(depth):
-        finish(s, s).start()
+    finish(0, 0).start()
     for load in loads:
         load.wait()
 
@@ -289,7 +296,7 @@
                 for c in range(2):
                     buf[t, e, c] = both[16 * t : 16 * t + 16, 128 * c : 128 * c + 128]
 
-    def coherence(p, buf, grid, slot):
+    def coherence(p, buf, grid):
         lines, tiles = [], []
         for t in range(10):
             fields = [[], [], [], []]
@@ -301,10 +308,12 @@
                 fields[2].append(ar * ar + ai * ai)
                 fields[3].append(br * br + bi * bi)
             tiles.append(fields)
-            if t >= 2:
-                for k in range(4):
-                    three = [tiles[t - 2][k][e] + tiles[t - 1][k][e] + tiles[t][k][e] for e in range(2)]
-                    lines.append(jnp.concatenate(three, 1))
+            if t >= 3 and t % 2:
+                inner = [[tiles[t - 2][k][e] + tiles[t - 1][k][e] for e in range(2)] for k in range(4)]
+                for o in (t - 3, t):
+                    for k in range(4):
+                        three = [inner[k][e] + tiles[o][k][e] for e in range(2)]
+                        lines.append(jnp.concatenate(three, 1))
         looked = jnp.dot(jnp.concatenate(lines, 0), win[...], preferred_element_type=F32)
         for t in range(8):
             cr, ci, pr, ps = (looked[64 * t + 16 * k : 64 * t + 16 * k + 16] for k in range(4))
@@ -315,31 +324,39 @@
                     for g in range(2):
                         where = pl.ds(8 * PITCH * g + t, 8, stride=PITCH)
                         grid[2 * c + h, where, :] = v[8 * g : 8 * g + 8, 128 * h : 128 * h + 128]
+
+    def emit(grid, slot):
         for q in range(4):
             for s in range(8):
                 v = [grid[q, pl.ds(PITCH * (2 * s + g), 8), :] for g in range(2)]
                 ready[slot, 16 * s : 16 * s + 16, 128 * q : 128 * q + 128] = jnp.concatenate(v, 0).astype(BF16)
 
-    secs, grids = (sec0, sec1), (grid0, grid1)
+    secs, grids = (sec0, sec1), (grid0, grid1, grid2, grid3)
+    groups = pairs // unroll
+    last = grids[(unroll - 1) % 4]
     secondary(0, sec0)
 
-    @pl.loop(0, pairs // unroll)
+    @pl.loop(0, groups)
     def _(i):
         base = unroll * i
-        at = [lax.rem(base + u, depth) for u in range(unroll)]
-        for u in range(unroll):
-            finish(base + u, at[u]).wait()
+        half = lax.rem(i, 2)
+        finish(i, half).wait()
+        emit(last, unroll * (1 - half) + unroll - 1)
+        finish(lax.rem(i + groups - 1, groups), 1 - half).start()
         for u in range(unroll):
             following = base + u + 1
             if u == unroll - 1:
                 following = jnp.minimum(following, pairs - 1)
             secondary(following, secs[(u + 1) % 2])
-            coherence(base + u, secs[u % 2], grids[u % 2], at[u])
-        for u in range(unroll):
-            finish(base + u, at[u]).start()
-
-    for s in range(depth):
-        finish(s, s).wait()
+            coherence(base + u, secs[u % 2], grids[u % 4])
+            if u:
+                emit(grids[(u - 1) % 4], unroll * half + u - 1)
+
+    end = (groups - 1) % 2
+    emit(last, unroll * end + unroll - 1)
+    finish(groups - 1, end).start()
+    for half in range(2):
+        finish(0, half).wait()
 
 
 def local(acquisitions, partner, pair_count, band_low, band_high):
@@ -379,6 +396,7 @@
             pltpu.VMEM((4, dates, cols), BF16),
             pltpu.VMEM((4, dates, cols), F32),
             pltpu.VMEM((dates, quarters, BASE + 16 * PITCH + 8, 128), F32),
+            pltpu.VMEM((dates, quarters, BASE + 16 * PITCH + 8, 128), F32),
             pltpu.SemaphoreType.DMA((7,)),
             pltpu.SemaphoreType.DMA((5,)),
             pltpu.SemaphoreType.DMA((5,)),
@@ -388,9 +406,9 @@
         ),
         name="front",
     )(acquisitions, forward, even, odd, band_low, band_high, pair_count)
-    return pl.pallas_call(
+    pairs = pl.pallas_call(
         pair_kernel,
-        out_shape=jax.ShapeDtypeStruct((dates, slots, rows, cols), BF16),
+        out_shape=jax.ShapeDtypeStruct((dates * slots, rows, cols), BF16),
         in_specs=[vmem, vmem] + [hbm] * 7,
         out_specs=hbm,
         scratch_shapes=[
@@ -403,15 +421,15 @@
             pltpu.SMEM(pair_count.shape, jnp.int32),
             pltpu.VMEM((10, 2, 2, 16, 128), F32),
             pltpu.VMEM((10, 2, 2, 16, 128), F32),
-            pltpu.VMEM((quarters, 160, 128), F32),
-            pltpu.VMEM((quarters, 160, 128), F32),
+            *[pltpu.VMEM((quarters, 160, 128), F32)] * 4,
             pltpu.VMEM((2 * unroll, rows, cols), BF16),
             pltpu.SemaphoreType.DMA((7,)),
-            pltpu.SemaphoreType.DMA((2 * unroll,)),
+            pltpu.SemaphoreType.DMA((2,)),
         ],
         compiler_params=pltpu.CompilerParams(vmem_limit_bytes=16 << 20),
         name="pairs",
     )(far, ref, even, odd, window, partner, band_low, band_high, pair_count)
+    return pairs.reshape(dates, slots, rows, cols)
 
 
 def solution(mesh):

time: 32.4 us -> 26.7 us (0.82)
  Pallas kernels: 32.2 us -> 26.6 us
    pallas_call x1, Pallas kernels: 15.6 us -> 11.5 us  [local(): pl.pallas_call(front_kernel, out_shape=(jax.ShapeDtypeStruct((dates, quar...]
    pallas_call x1, Pallas kernels: 16.7 us -> 15 us  [local(): pl.pallas_call(pair_kernel, out_shape=jax.ShapeDtypeStruct((dates * slots...]
where the time goes in v2:
time: 26.7 us; the launch traced here: 26.6 us
  Pallas kernels  26.6 us (100%)
    pallas_call x1, Pallas kernels, local(): pl.pallas_call(pair_kernel, out_shape=jax.ShapeDtypeStruct((dates * slots...  15 us
    pallas_call x1, Pallas kernels, local(): pl.pallas_call(front_kernel, out_shape=(jax.ShapeDtypeStruct((dates, quar...  11.5 us

profile of v2, /device:TPU:97, one launch (start us, length us, event | category | flops | bytes accessed | tf_op | source)
XLA Modules:
  0.0 26.6 jit_solution(10532231996753569931)
XLA Ops:
  0.0 11.5 %front.1 = (f32[8,4,160,128]{3,2,1,0:T(8,128)S(1)}, f32[72,10,2,2,16,128]{5,4,3,2,1,0:T(8,128)S(1)}) custom-call(bf16[8,128,512]{2,1,0:T(8,128)(2,1)} %acq_hbm.1, bf16[512,512]{1,0:T(8,128)(2,1)} %constant.8.clone.fwd_hbm, bf16[256,256]{1,0:T(8,128)(2,1)} %constant.9.clone.even_hbm, bf16[256,256]{1,0:T(8,128)(2,1)} %constant.10.clone.odd_hbm, ...), custom_call_target="tpu_custom_call" | custom-call | tf_op jit(solution)/shard_map/front/pallas_call | solution.py:377
  11.5 15.0 %pairs.1 = bf16[72,128,512]{2,1,0:T(8,128)(2,1)} custom-call(f32[8,4,160,128]{3,2,1,0:T(8,128)S(1)} %get-tuple-element.7.far_ref, f32[72,10,2,2,16,128]{5,4,3,2,1,0:T(8,128)S(1)} %get-tuple-element.8.ref_ref, bf16[256,256]{1,0:T(8,128)(2,1)} %constant.9.clone.even_hbm, bf16[256,256]{1,0:T(8,128)(2,1)} %constant.10.clone.odd_hbm, ...), custom_call_target="tpu_custom_call" | custom-call | tf_op jit(solution)/shard_map/pairs/pallas_call | solution.py:409

commit v3 on v2

v3 whole, which is shorter than its diff:
```python
import functools
import math

import jax
import jax.numpy as jnp
import numpy as np
from jax import lax
from jax.experimental import pallas as pl
from jax.experimental.pallas import tpu as pltpu
from jax.sharding import PartitionSpec as P

F32 = jnp.float32
BF16 = jnp.bfloat16


def tables(bins):
    ids = np.arange(bins)
    angles = (ids[:, None] * ids[None, :] % bins) * (2.0 * math.pi / bins)
    cosine, sine = np.cos(angles), np.sin(angles)
    forward = np.block([[cosine, -sine], [sine, cosine]])
    inverse = np.block([[cosine, sine], [-sine, cosine]]) / bins
    half = bins // 2
    rows = np.concatenate([np.arange(half), bins + np.arange(half)])
    even = np.concatenate([np.arange(0, bins, 2), bins + np.arange(0, bins, 2)])
    odd = even + 1
    order = np.concatenate([np.arange(0, bins, 2), np.arange(1, bins, 2)])
    window = (np.abs(order[:, None] - ids[None, :]) <= 4).astype(np.float32)
    return (
        jnp.asarray(forward, BF16),
        jnp.asarray(inverse[rows][:, even], BF16),
        jnp.asarray(inverse[rows][:, odd], BF16),
        jnp.asarray(window, BF16),
    )


PITCH = 9
MESH = pl.DeviceIdType.MESH


def segment(ref, lead, t):
    parts = [ref[lead + (pl.ds(8 * PITCH * h + t, 8, stride=PITCH),)] for h in range(2)]
    return jnp.concatenate(parts, 0)


def inside(low, high):
    lane = lax.broadcasted_iota(jnp.int32, (16, 128), 1)
    return [
        ((lane + shift >= low) & (lane + shift < high)).astype(F32).astype(BF16)
        for shift in (0, 128)
    ]


def halves(tile, masks):
    x = [tile[q] * masks[q % 2] for q in range(4)]
    return (
        jnp.concatenate([x[0] + x[1], x[2] + x[3]], 1),
        jnp.concatenate([x[0] - x[1], x[2] - x[3]], 1),
    )


def front_kernel(
    acq_hbm, fwd_hbm, even_hbm, odd_hbm, win_hbm, partner_hbm, low_hbm, high_hbm, count_hbm,
    ref_ref, sec_ref, rim_ref, win_ref,
    own, other, fwd, even, odd, partner_s, low_s, high_s, count_s,
    edge_f, edge, halo, halo_f, picked, nat, nat_far, local_sem, send, recv,
):
    dates, rows, cols = own.shape
    slots = low_s.shape[1]
    quarters = cols // 128
    date = lax.axis_index("date")
    space = lax.axis_index("space")
    count = lax.axis_size("space")
    before = lax.rem(space + count - 1, count)
    after = lax.rem(space + 1, count)
    far = 1 - date
    has_before = space > 0
    has_after = space < count - 1

    barrier = pltpu.get_barrier_semaphore()

    def greet(peer):
        pl.semaphore_signal(barrier, inc=1, device_id=peer, device_id_type=MESH)

    greet((far, space))

    @pl.when(has_before)
    def _():
        greet((date, before))
        greet((far, before))

    @pl.when(has_after)
    def _():
        greet((date, after))
        greet((far, after))

    loads = [
        pltpu.make_async_copy(src, dst, local_sem.at[k])
        for k, (src, dst) in enumerate(
            (
                (acq_hbm, own),
                (fwd_hbm, fwd),
                (even_hbm, even),
                (odd_hbm, odd),
                (low_hbm, low_s),
                (high_hbm, high_s),
                (count_hbm, count_s),
                (partner_hbm, partner_s),
                (win_hbm, win_ref),
            )
        )
    ]
    for load in loads:
        load.start()

    def remote(src, dst, k, peer):
        return pltpu.make_async_remote_copy(
            src_ref=src,
            dst_ref=dst,
            send_sem=send.at[k],
            recv_sem=recv.at[k],
            device_id=peer,
            device_id_type=MESH,
        )

    down = [remote(edge.at[1], halo.at[0], 0, (date, after)), remote(edge.at[1], halo.at[2], 2, (far, after))]
    up = [remote(edge.at[0], halo.at[1], 1, (date, before)), remote(edge.at[0], halo.at[3], 3, (far, before))]
    big = remote(own, other, 4, (far, space))

    loads[0].wait()
    for d in range(dates):
        edge_f[0, d : d + 1, :] = own[d, 0:16, :].astype(F32)[0:1]
        edge_f[1, d : d + 1, :] = own[d, rows - 16 : rows, :].astype(F32)[15:16]
    edge[...] = edge_f[...].astype(BF16)

    pl.semaphore_wait(
        barrier, 1 + 2 * has_before.astype(jnp.int32) + 2 * has_after.astype(jnp.int32)
    )

    @pl.when(has_after)
    def _():
        for copy in down:
            copy.start()

    @pl.when(has_before)
    def _():
        for copy in up:
            copy.start()

    big.start()

    def transform(source, target):
        block = jnp.dot(
            source[...].reshape(dates * rows, cols), fwd[...], preferred_element_type=F32
        )
        for i in range(dates):
            for s in range(rows // 8):
                top = i * rows + 8 * s
                place = slice(PITCH * s, PITCH * s + 8)
                for q in range(quarters):
                    target[i, q, place, :] = block[top : top + 8, q * 128 : q * 128 + 128]

    first = date * dates
    steps = rows // 16

    def read(source, index):
        return [[segment(source, (index, q), t).astype(BF16) for q in range(quarters)] for t in range(steps)]

    def limits(i, j):
        return jnp.where(j < count_s[first + i], low_s[i, j], 512), high_s[i, j]

    def chosen(i, j):
        return lax.rem(partner_s[first + i, j], dates)

    def products(start, amount, out, spectra):
        plus, minus = [], []
        for n in range(amount):
            for j in range(slots):
                masks = inside(*limits(start + n, j))
                for tile in spectra(n, j):
                    p, m = halves(tile, masks)
                    plus.append(p)
                    minus.append(m)
        for e, (part, table) in enumerate(((plus, even), (minus, odd))):
            both = jnp.dot(jnp.concatenate(part, 0), table[...], preferred_element_type=F32)
            for n in range(amount * slots):
                for c in range(2):
                    out[start * slots + n, e, c] = both[rows * n : rows * n + rows, 128 * c : 128 * c + 128]

    def references(start, amount):
        x = [read(nat, start + n) for n in range(amount)]
        products(start, amount, ref_ref, lambda n, j: x[n])

    def secondaries(start, amount):
        products(start, amount, sec_ref, lambda n, j: read(nat_far, chosen(start + n, j)))

    for load in loads[1:]:
        load.wait()

    transform(own, nat)

    @pl.loop(0, dates // 2)
    def _(i):
        references(2 * i, 2)

    big.wait()
    transform(other, nat_far)

    @pl.loop(0, dates // 2)
    def _(i):
        secondaries(2 * i, 2)

    @pl.when(has_after)
    def _():
        for copy in down:
            copy.wait_send()
        for copy in up:
            copy.wait_recv()

    @pl.when(has_before)
    def _():
        for copy in up:
            copy.wait_send()
        for copy in down:
            copy.wait_recv()

    @pl.when(jnp.logical_not(has_before))
    def _():
        halo[0] = jnp.zeros(halo.shape[1:], BF16)
        halo[2] = jnp.zeros(halo.shape[1:], BF16)

    @pl.when(jnp.logical_not(has_after))
    def _():
        halo[1] = jnp.zeros(halo.shape[1:], BF16)
        halo[3] = jnp.zeros(halo.shape[1:], BF16)

    halo_f[...] = jnp.dot(
        halo[...].reshape(4 * dates, cols), fwd[...], preferred_element_type=F32
    ).reshape(4, dates, cols)
    for j in range(slots):
        for d in range(dates):
            index = chosen(d, j)
            for k in range(2):
                picked[j, dates * k + d : dates * k + d + 1, :] = halo_f[2 + k, pl.ds(index, 1), :]
    row = lax.rem(lax.broadcasted_iota(jnp.int32, (16, 128), 0), dates)
    masks = []
    for j in range(slots):
        low = high = jnp.zeros((16, 128), jnp.int32)
        for d in range(dates):
            one_low, one_high = limits(d, j)
            low = jnp.where(row == d, one_low, low)
            high = jnp.where(row == d, one_high, high)
        masks.append(inside(low, high))
    near = jnp.concatenate([halo_f[0], halo_f[1]], 0).astype(BF16)
    for k in range(2):
        plus, minus = [], []
        for j in range(slots):
            line = picked[j].astype(BF16) if k else near
            p, m = halves([line[:, 128 * q : 128 * q + 128] for q in range(quarters)], masks[j])
            plus.append(p)
            minus.append(m)
        for e, (part, table) in enumerate(((plus, even), (minus, odd))):
            both = jnp.dot(jnp.concatenate(part, 0), table[...], preferred_element_type=F32)
            for c in range(2):
                rim_ref[k, e, c] = both[:, 128 * c : 128 * c + 128]


def pair_kernel(ref_ref, sec_ref, rim_ref, win, out_ref, grid0, grid1, grid2, grid3, ready, out_sem):
    pairs = ref_ref.shape[0]
    dates = 8
    slots = pairs // dates
    sublane = lax.broadcasted_iota(jnp.int32, (8, 128), 0)
    banks, splits = out_sem.shape
    unroll = ready.shape[0] // banks
    part = unroll // splits
    groups = pairs // unroll

    def finish(group, bank):
        return [
            pltpu.make_async_copy(
                ready.at[pl.ds(unroll * bank + part * k, part)],
                out_ref.at[pl.ds(unroll * group + part * k, part)],
                out_sem.at[bank, k],
            )
            for k in range(splits)
        ]

    def start(copies):
        for copy in copies:
            copy.start()

    def wait(copies):
        for copy in copies:
            copy.wait()

    for bank in range(banks - 1):
        start(finish(bank, bank))

    def field(ref, k, p, t, e, c):
        if 0 <= t < 8:
            return ref[p, e, c, 16 * t : 16 * t + 16, :].astype(BF16)
        d = p // slots
        line = 2 * dates * (p - d * slots) + d
        if t < 0:
            low = ref[p, e, c, pl.ds(111, 8), :]
            low = jnp.where(sublane == 0, rim_ref[k, e, c, pl.ds(line, 1), :], low)
            high = ref[p, e, c, pl.ds(119, 8), :]
        else:
            low = ref[p, e, c, pl.ds(1, 8), :]
            high = ref[p, e, c, pl.ds(9, 8), :]
            high = jnp.where(sublane == 7, rim_ref[k, e, c, pl.ds(line + dates, 1), :], high)
        return jnp.concatenate([low, high], 0).astype(BF16)

    def coherence(p, grid):
        lines, tiles = [], []
        for t in range(10):
            fields = [[], [], [], []]
            for e in range(2):
                ar, ai = (field(ref_ref, 0, p, t - 1, e, c) for c in range(2))
                br, bi = (field(sec_ref, 1, p, t - 1, e, c) for c in range(2))
                fields[0].append(ar * br + ai * bi)
                fields[1].append(ai * br - ar * bi)
                fields[2].append(ar * ar + ai * ai)
                fields[3].append(br * br + bi * bi)
            tiles.append(fields)
            if t >= 3 and t % 2:
                inner = [[tiles[t - 2][k][e] + tiles[t - 1][k][e] for e in range(2)] for k in range(4)]
                for o in (t - 3, t):
                    for k in range(4):
                        three = [inner[k][e] + tiles[o][k][e] for e in range(2)]
                        lines.append(jnp.concatenate(three, 1))
        looked = jnp.dot(jnp.concatenate(lines, 0), win[...], preferred_element_type=F32)
        for t in range(8):
            cr, ci, pr, ps = (looked[64 * t + 16 * k : 64 * t + 16 * k + 16] for k in range(4))
            norm = lax.rsqrt(jnp.maximum(pr, 1.0) * jnp.maximum(ps, 1.0))
            for c, v in ((0, cr), (1, ci)):
                v = v * norm
                for h in range(2):
                    for g in range(2):
                        where = pl.ds(8 * PITCH * g + t, 8, stride=PITCH)
                        grid[2 * c + h, where, :] = v[8 * g : 8 * g + 8, 128 * h : 128 * h + 128]

    def emit(grid, slot):
        for q in range(4):
            for s in range(8):
                v = [grid[q, pl.ds(PITCH * (2 * s + g), 8), :] for g in range(2)]
                ready[slot, 16 * s : 16 * s + 16, 128 * q : 128 * q + 128] = jnp.concatenate(v, 0).astype(BF16)

    grids = (grid0, grid1, grid2, grid3)
    last = grids[(unroll - 1) % 4]

    @pl.loop(0, groups)
    def _(i):
        bank = lax.rem(i, banks)
        previous = lax.rem(i + banks - 1, banks)
        wait(finish(i, bank))
        emit(last, unroll * previous + unroll - 1)
        start(finish(lax.rem(i + groups - 1, groups), previous))
        for u in range(unroll):
            coherence(unroll * i + u, grids[u % 4])
            if u:
                emit(grids[(u - 1) % 4], unroll * bank + u - 1)

    end = (groups - 1) % banks
    emit(last, unroll * end + unroll - 1)
    start(finish(groups - 1, end))
    for bank in range(banks):
        wait(finish(0, bank))


def local(acquisitions, partner, pair_count, band_low, band_high):
    dates, rows, cols = acquisitions.shape
    slots = partner.shape[1]
    quarters = cols // 128
    unroll = 8
    forward, even, odd, window = tables(cols // 2)
    vmem = pl.BlockSpec(memory_space=pltpu.VMEM)
    hbm = pl.BlockSpec(memory_space=pltpu.HBM)
    stay = functools.partial(pltpu.with_memory_space_constraint, memory_space=pltpu.HBM)
    forward, even, odd, window, acquisitions, partner, pair_count, band_low, band_high = (
        stay(x)
        for x in (forward, even, odd, window, acquisitions, partner, pair_count, band_low, band_high)
    )
    half = pltpu.VMEM((256, 256), BF16)
    per_slot = pltpu.SMEM((dates, slots), jnp.int32)
    fields = jax.ShapeDtypeStruct((dates * slots, 2, 2, rows, 128), F32)
    rim_shape = jax.ShapeDtypeStruct((2, 2, 2, 2 * dates * slots, 128), F32)
    natural = pltpu.VMEM((dates, quarters, 16 * PITCH, 128), F32)
    ref, sec, rim, win = pl.pallas_call(
        front_kernel,
        out_shape=(fields, fields, rim_shape, jax.ShapeDtypeStruct(window.shape, BF16)),
        in_specs=[hbm] * 9,
        out_specs=(vmem, vmem, vmem, vmem),
        scratch_shapes=[
            pltpu.VMEM((dates, rows, cols), BF16),
            pltpu.VMEM((dates, rows, cols), BF16),
            pltpu.VMEM((cols, cols), BF16),
            half,
            half,
            pltpu.SMEM(partner.shape, jnp.int32),
            per_slot,
            per_slot,
            pltpu.SMEM(pair_count.shape, jnp.int32),
            pltpu.VMEM((2, dates, cols), F32),
            pltpu.VMEM((2, dates, cols), BF16),
            pltpu.VMEM((4, dates, cols), BF16),
            pltpu.VMEM((4, dates, cols), F32),
            pltpu.VMEM((slots, 2 * dates, cols), F32),
            natural,
            natural,
            pltpu.SemaphoreType.DMA((9,)),
            pltpu.SemaphoreType.DMA((5,)),
            pltpu.SemaphoreType.DMA((5,)),
        ],
        compiler_params=pltpu.CompilerParams(
            collective_id=0, has_side_effects=True, vmem_limit_bytes=14 << 20
        ),
        name="front",
    )(acquisitions, forward, even, odd, window, partner, band_low, band_high, pair_count)
    pairs = pl.pallas_call(
        pair_kernel,
        out_shape=jax.ShapeDtypeStruct((dates * slots, rows, cols), BF16),
        in_specs=[vmem, vmem, vmem, vmem],
        out_specs=hbm,
        scratch_shapes=[
            *[pltpu.VMEM((quarters, 160, 128), F32)] * 4,
            pltpu.VMEM((3 * unroll, rows, cols), BF16),
            pltpu.SemaphoreType.DMA((3, 4)),
        ],
        compiler_params=pltpu.CompilerParams(vmem_limit_bytes=14 << 20),
        name="pairs",
    )(ref, sec, rim, win)
    return pairs.reshape(dates, slots, rows, cols)


def solution(mesh):
    placed = (P("date", "space", None), P(), P(), P("date", None), P("date", None))
    return jax.shard_map(
        local, mesh=mesh, in_specs=placed, out_specs=P("date", None, "space", None), check_vma=False
    )
```

time: 26.7 us -> 27 us (1.011)
  Pallas kernels: 26.6 us -> 26.9 us
    pallas_call x1, Pallas kernels: 11.5 us -> 13.9 us  [local(): pl.pallas_call(front_kernel, out_shape=(fields, fields, rim_shape, jax.Sh...]
    pallas_call x1, Pallas kernels: 15 us -> 13 us  [local(): pl.pallas_call(pair_kernel, out_shape=jax.ShapeDtypeStruct((dates * slots...]
where the time goes in v3:
time: 27 us; the launch traced here: 26.9 us
  Pallas kernels  26.9 us (100%)
    pallas_call x1, Pallas kernels, local(): pl.pallas_call(front_kernel, out_shape=(fields, fields, rim_shape, jax.Sh...  13.9 us
    pallas_call x1, Pallas kernels, local(): pl.pallas_call(pair_kernel, out_shape=jax.ShapeDtypeStruct((dates * slots...  13 us

profile of v3, /device:TPU:97, one launch (start us, length us, event | category | flops | bytes accessed | tf_op | source)
XLA Modules:
  0.0 26.9 jit_solution(11927248430439631014)
XLA Ops:
  0.0 13.9 %front.1 = (f32[72,2,2,128,128]{4,3,2,1,0:T(8,128)S(1)}, f32[72,2,2,128,128]{4,3,2,1,0:T(8,128)S(1)}, f32[2,2,2,144,128]{4,3,2,1,0:T(8,128)S(1)}, bf16[256,256]{1,0:T(8,128)(2,1)S(1)}) custom-call(bf16[8,128,512]{2,1,0:T(8,128)(2,1)} %acq_hbm.1, bf16[512,512]{1,0:T(8,128)(2,1)} %constant.8.clone.fwd_hbm, bf16[256,256]{1,0:T(8,128)(2,1)} %constant.9.clone.even_hbm, ...), custom_call_target="tpu_custom_call" | custom-call | tf_op jit(solution)/shard_map/front/pallas_call | solution.py:388
  13.9 13.0 %pairs.1 = bf16[72,128,512]{2,1,0:T(8,128)(2,1)} custom-call(f32[72,2,2,128,128]{4,3,2,1,0:T(8,128)S(1)} %get-tuple-element.9.ref_ref, f32[72,2,2,128,128]{4,3,2,1,0:T(8,128)S(1)} %get-tuple-element.10.sec_ref, f32[2,2,2,144,128]{4,3,2,1,0:T(8,128)S(1)} %get-tuple-element.11.rim_ref, bf16[256,256]{1,0:T(8,128)(2,1)S(1)} %get-tuple-element.12.win), custom_call_target="tpu_custom_call" | custom-call | tf_op jit(solution)/shard_map/pairs/pallas_call | solution.py:419

commit v4 on v3

--- a/solution.py
+++ b/solution.py
@@ -132,22 +132,6 @@
         edge_f[1, d : d + 1, :] = own[d, rows - 16 : rows, :].astype(F32)[15:16]
     edge[...] = edge_f[...].astype(BF16)
 
-    pl.semaphore_wait(
-        barrier, 1 + 2 * has_before.astype(jnp.int32) + 2 * has_after.astype(jnp.int32)
-    )
-
-    @pl.when(has_after)
-    def _():
-        for copy in down:
-            copy.start()
-
-    @pl.when(has_before)
-    def _():
-        for copy in up:
-            copy.start()
-
-    big.start()
-
     def transform(source, target):
         block = jnp.dot(
             source[...].reshape(dates * rows, cols), fwd[...], preferred_element_type=F32
@@ -198,7 +182,27 @@
 
     transform(own, nat)
 
-    @pl.loop(0, dates // 2)
+    @pl.loop(0, dates // 4)
+    def _(i):
+        references(2 * i, 2)
+
+    pl.semaphore_wait(
+        barrier, 1 + 2 * has_before.astype(jnp.int32) + 2 * has_after.astype(jnp.int32)
+    )
+
+    @pl.when(has_after)
+    def _():
+        for copy in down:
+            copy.start()
+
+    @pl.when(has_before)
+    def _():
+        for copy in up:
+            copy.start()
+
+    big.start()
+
+    @pl.loop(dates // 4, dates // 2)
     def _(i):
         references(2 * i, 2)
 

time: 27 us -> 25.6 us (0.948)
  Pallas kernels: 26.9 us -> 25.5 us
    pallas_call x1, Pallas kernels: 13.9 us -> 12.5 us  [local(): pl.pallas_call(front_kernel, out_shape=(fields, fields, rim_shape, jax.Sh...]
where the time goes in v4:
time: 25.6 us; the launch traced here: 25.5 us
  Pallas kernels  25.5 us (100%)
    pallas_call x1, Pallas kernels, local(): pl.pallas_call(pair_kernel, out_shape=jax.ShapeDtypeStruct((dates * slots...  13 us
    pallas_call x1, Pallas kernels, local(): pl.pallas_call(front_kernel, out_shape=(fields, fields, rim_shape, jax.Sh...  12.5 us

profile of v4, /device:TPU:97, one launch (start us, length us, event | category | flops | bytes accessed | tf_op | source)
XLA Modules:
  0.0 25.5 jit_solution(10452337041885431137)
XLA Ops:
  0.0 12.5 %front.1 = (f32[72,2,2,128,128]{4,3,2,1,0:T(8,128)S(1)}, f32[72,2,2,128,128]{4,3,2,1,0:T(8,128)S(1)}, f32[2,2,2,144,128]{4,3,2,1,0:T(8,128)S(1)}, bf16[256,256]{1,0:T(8,128)(2,1)S(1)}) custom-call(bf16[8,128,512]{2,1,0:T(8,128)(2,1)} %acq_hbm.1, bf16[512,512]{1,0:T(8,128)(2,1)} %constant.8.clone.fwd_hbm, bf16[256,256]{1,0:T(8,128)(2,1)} %constant.9.clone.even_hbm, ...), custom_call_target="tpu_custom_call" | custom-call | tf_op jit(solution)/shard_map/front/pallas_call | solution.py:392
  12.5 13.0 %pairs.1 = bf16[72,128,512]{2,1,0:T(8,128)(2,1)} custom-call(f32[72,2,2,128,128]{4,3,2,1,0:T(8,128)S(1)} %get-tuple-element.9.ref_ref, f32[72,2,2,128,128]{4,3,2,1,0:T(8,128)S(1)} %get-tuple-element.10.sec_ref, f32[2,2,2,144,128]{4,3,2,1,0:T(8,128)S(1)} %get-tuple-element.11.rim_ref, bf16[256,256]{1,0:T(8,128)(2,1)S(1)} %get-tuple-element.12.win), custom_call_target="tpu_custom_call" | custom-call | tf_op jit(solution)/shard_map/pairs/pallas_call | solution.py:423

commit v5 on v4

--- a/solution.py
+++ b/solution.py
@@ -124,7 +124,11 @@
 
     down = [remote(edge.at[1], halo.at[0], 0, (date, after)), remote(edge.at[1], halo.at[2], 2, (far, after))]
     up = [remote(edge.at[0], halo.at[1], 1, (date, before)), remote(edge.at[0], halo.at[3], 3, (far, before))]
-    big = remote(own, other, 4, (far, space))
+    chunk = dates // 2
+    big = [
+        remote(own.at[pl.ds(chunk * k, chunk)], other.at[pl.ds(chunk * k, chunk)], 4 + k, (far, space))
+        for k in range(2)
+    ]
 
     loads[0].wait()
     for d in range(dates):
@@ -132,13 +136,13 @@
         edge_f[1, d : d + 1, :] = own[d, rows - 16 : rows, :].astype(F32)[15:16]
     edge[...] = edge_f[...].astype(BF16)
 
-    def transform(source, target):
+    def transform(source, target, start, amount):
         block = jnp.dot(
-            source[...].reshape(dates * rows, cols), fwd[...], preferred_element_type=F32
+            source[start : start + amount].reshape(amount * rows, cols), fwd[...], preferred_element_type=F32
         )
-        for i in range(dates):
+        for i in range(start, start + amount):
             for s in range(rows // 8):
-                top = i * rows + 8 * s
+                top = (i - start) * rows + 8 * s
                 place = slice(PITCH * s, PITCH * s + 8)
                 for q in range(quarters):
                     target[i, q, place, :] = block[top : top + 8, q * 128 : q * 128 + 128]
@@ -180,7 +184,7 @@
     for load in loads[1:]:
         load.wait()
 
-    transform(own, nat)
+    transform(own, nat, 0, dates)
 
     @pl.loop(0, dates // 4)
     def _(i):
@@ -200,14 +204,16 @@
         for copy in up:
             copy.start()
 
-    big.start()
+    for copy in big:
+        copy.start()
 
     @pl.loop(dates // 4, dates // 2)
     def _(i):
         references(2 * i, 2)
 
-    big.wait()
-    transform(other, nat_far)
+    for k in range(2):
+        big[k].wait()
+        transform(other, nat_far, chunk * k, chunk)
 
     @pl.loop(0, dates // 2)
     def _(i):
@@ -296,8 +302,8 @@
         for copy in copies:
             copy.wait()
 
-    for bank in range(banks - 1):
-        start(finish(bank, bank))
+    for bank in range(banks):
+        start(finish(bank, bank)[: splits - 1 if bank == banks - 1 else splits])
 
     def field(ref, k, p, t, e, c):
         if 0 <= t < 8:
@@ -358,15 +364,17 @@
         previous = lax.rem(i + banks - 1, banks)
         wait(finish(i, bank))
         emit(last, unroll * previous + unroll - 1)
-        start(finish(lax.rem(i + groups - 1, groups), previous))
+        start(finish(lax.rem(i + groups - 1, groups), previous)[splits - 1 :])
         for u in range(unroll):
             coherence(unroll * i + u, grids[u % 4])
             if u:
                 emit(grids[(u - 1) % 4], unroll * bank + u - 1)
+                if u % part == 0:
+                    start(finish(i, bank)[u // part - 1 : u // part])
 
     end = (groups - 1) % banks
     emit(last, unroll * end + unroll - 1)
-    start(finish(groups - 1, end))
+    start(finish(groups - 1, end)[splits - 1 :])
     for bank in range(banks):
         wait(finish(0, bank))
 
@@ -412,8 +420,8 @@
             natural,
             natural,
             pltpu.SemaphoreType.DMA((9,)),
-            pltpu.SemaphoreType.DMA((5,)),
-            pltpu.SemaphoreType.DMA((5,)),
+            pltpu.SemaphoreType.DMA((6,)),
+            pltpu.SemaphoreType.DMA((6,)),
         ],
         compiler_params=pltpu.CompilerParams(
             collective_id=0, has_side_effects=True, vmem_limit_bytes=14 << 20

time: 25.6 us -> 25.1 us (0.980)
  Pallas kernels: 25.5 us -> 24.9 us
    pallas_call x1, Pallas kernels: 13 us -> 12.7 us  [local(): pl.pallas_call(pair_kernel, out_shape=jax.ShapeDtypeStruct((dates * slots...]
where the time goes in v5:
time: 25.1 us; the launch traced here: 25 us
  Pallas kernels  24.9 us (99%)
    pallas_call x1, Pallas kernels, local(): pl.pallas_call(pair_kernel, out_shape=jax.ShapeDtypeStruct((dates * slots...  12.7 us
    pallas_call x1, Pallas kernels, local(): pl.pallas_call(front_kernel, out_shape=(fields, fields, rim_shape, jax.Sh...  12.3 us

profile of v5, /device:TPU:97, one launch (start us, length us, event | category | flops | bytes accessed | tf_op | source)
XLA Modules:
  0.0 25.0 jit_solution(6002359069667385213)
XLA Ops:
  0.0 12.3 %front.1 = (f32[72,2,2,128,128]{4,3,2,1,0:T(8,128)S(1)}, f32[72,2,2,128,128]{4,3,2,1,0:T(8,128)S(1)}, f32[2,2,2,144,128]{4,3,2,1,0:T(8,128)S(1)}, bf16[256,256]{1,0:T(8,128)(2,1)S(1)}) custom-call(bf16[8,128,512]{2,1,0:T(8,128)(2,1)} %acq_hbm.1, bf16[512,512]{1,0:T(8,128)(2,1)} %constant.8.clone.fwd_hbm, bf16[256,256]{1,0:T(8,128)(2,1)} %constant.9.clone.even_hbm, ...), custom_call_target="tpu_custom_call" | custom-call | tf_op jit(solution)/shard_map/front/pallas_call | solution.py:400
  12.3 12.7 %pairs.1 = bf16[72,128,512]{2,1,0:T(8,128)(2,1)} custom-call(f32[72,2,2,128,128]{4,3,2,1,0:T(8,128)S(1)} %get-tuple-element.9.ref_ref, f32[72,2,2,128,128]{4,3,2,1,0:T(8,128)S(1)} %get-tuple-element.10.sec_ref, f32[2,2,2,144,128]{4,3,2,1,0:T(8,128)S(1)} %get-tuple-element.11.rim_ref, bf16[256,256]{1,0:T(8,128)(2,1)S(1)} %get-tuple-element.12.win), custom_call_target="tpu_custom_call" | custom-call | tf_op jit(solution)/shard_map/pairs/pallas_call | solution.py:431
